TPU v7x, 32 devices: a whole 2x2x4 slice. The times are simulated.
32 devices in a mesh: groups: 1, local: 32 (over z, y, x, core).
Axes of the slice: x: 2, y: 2, z: 4, core: 2. Of those that a mesh axis runs over, the one named last changes fastest.
Arguments:
- tokens: bfloat16 [2048, 2048], P(('groups', 'local')), may hold values from -6 to 6
- expert_ids: int32 [2048, 2], P(('groups', 'local')), may hold values from 0 to 3, all different within a row; in each aligned block of 64 rows (0 to 63, 64 to 127, ...) at most 48 rows name the same one
- gate_weights: float32 [2048, 2], P(('groups', 'local')), may hold values from 0.2 to 1
- norm_gain: float32 [2048], replicated, may hold values from 0.25 to 1.75
- norm_bias: float32 [2048], replicated, may hold values from -3 to 3
- w_in: bfloat16 [32, 2048, 1024], P('local'), may hold values from -0.125 to 0.125
- b_in: float32 [32, 1024], P('local'), may hold values from -4 to 4
- w_out: bfloat16 [32, 1024, 2048], P('local'), may hold values from -0.0625 to 0.0625
- b_out: float32 [4, 2048], replicated, may hold values from -3 to 3
Outputs:
- mixed_out: bfloat16 [2048, 2048], P(('groups', 'local'))
Inputs may be any that keep to these rules, and one draw needn't show every extreme that they name: `expert_ids`: among the 64 tokens of one device, no expert is named by more than 48 pairs, a bound that some block reaches; a token's 2 experts differ.
All inputs are finite; a program needn't handle non-finite values.
Results may differ from a plain program's by a relative error of at most 0.008.
Values may be sent and summed in bfloat16 or wider, within the bound.
A program may use at most 128 MiB of HBM per device.

v0:
```python
import functools

import jax
import jax.numpy as jnp
from jax import lax
from jax.experimental import pallas as pl
from jax.experimental.pallas import tpu as pltpu
from jax.sharding import PartitionSpec as P

MESH = pl.DeviceIdType.MESH
F32 = jnp.float32
BF16 = jnp.bfloat16
ZIN, OWN_A, OWN_B, OWN_P, FWD_B, FWD_P1, FWD_P2, FWD_P3, FWD_A = range(9)
PAIR, DIAG, ONE, TWO, BACK = 9, 11, 13, 15, 17
KINDS = 19


def xor_with(value, fixed, limit):
    out, bit = 0, 1
    while bit < limit:
        digit = lax.rem(lax.div(value, bit), 2)
        out = out + bit * ((1 - digit) if fixed & bit else digit)
        bit *= 2
    return out


def kernel(
    experts, cap, tokens_ref, idst_ref, gatest_ref, gain_ref, bias_ref, b_in_ref, b_out_ref,
    w_in_hbm, w_out_hbm, out_ref, w_in, w_out, rows, outbox, hidden, part, pair, diag, from_b, from_a,
    sums, back, returned, load_sems, send_sems, recv_sems,
):
    tok, width = tokens_ref.shape
    hid = hidden.shape[1]
    half = width // 2
    shared = 8
    me = lax.axis_index("local")
    plane = lax.div(me, shared)
    seat = lax.rem(me, shared)
    core = lax.rem(seat, 2)
    base = plane * shared
    seat_x = seat + 2 - 4 * lax.rem(lax.div(seat, 2), 2)
    seat_y = seat + 4 - 8 * lax.div(seat, 4)
    mate = base + seat + 1 - 2 * core
    near_a = base + seat_x + core * (seat_y - seat_x)
    near_b = base + seat_y + core * (seat_x - seat_y)
    planes = [xor_with(plane, j, experts) for j in range(experts)]
    others = [planes[j] * shared + seat for j in range(experts)]

    loads = [
        pltpu.make_async_copy(w_in_hbm.at[0], w_in, load_sems.at[0]),
        pltpu.make_async_copy(w_out_hbm.at[0], w_out, load_sems.at[1]),
    ]
    for load in loads:
        load.start()

    barrier = pltpu.get_barrier_semaphore()
    partners = [mate, near_a, near_b] + others[1:]
    for partner in partners:
        pl.semaphore_signal(barrier, inc=1, device_id={"local": partner}, device_id_type=MESH)

    def chunk(j, q, count=1):
        return rows.at[j, pl.ds(q * cap, count * cap)]

    def piece(j, q, at):
        return rows.at[j, pl.ds(q * cap, cap), at]

    def copy(j, kind, src, dst, target):
        return pltpu.make_async_remote_copy(
            src_ref=src, dst_ref=dst, send_sem=send_sems.at[j * KINDS + kind],
            recv_sem=recv_sems.at[j * KINDS + kind], device_id={"local": target}, device_id_type=MESH,
        )

    copies = {}
    for j in range(experts):
        if j:
            copies[j, ZIN] = copy(j, ZIN, outbox.at[j], chunk(j, 0), others[j])
        copies[j, OWN_A] = copy(j, OWN_A, chunk(j, 0), chunk(j, 1), near_a)
        copies[j, OWN_B] = copy(j, OWN_B, chunk(j, 0), chunk(j, 2), near_b)
        copies[j, OWN_P] = copy(j, OWN_P, chunk(j, 0), chunk(j, 4), mate)
        low, high = pl.ds(0, half), pl.ds(half, half)
        copies[j, FWD_B] = copy(j, FWD_B, piece(j, 1, low), piece(j, 3, low), near_b)
        copies[j, FWD_A] = copy(j, FWD_A, piece(j, 2, high), piece(j, 3, high), near_a)
        copies[j, FWD_P1] = copy(j, FWD_P1, chunk(j, 1), chunk(j, 5), mate)
        copies[j, FWD_P2] = copy(j, FWD_P2, chunk(j, 2), chunk(j, 6), mate)
        copies[j, FWD_P3] = copy(j, FWD_P3, chunk(j, 3), chunk(j, 7), mate)
        for h in range(2):
            at = pl.ds(h * half, half)
            every = pl.ds(0, cap)
            copies[j, PAIR + h] = copy(
                j, PAIR + h, part.at[j, pl.ds(4 * cap, 4 * cap), at], pair.at[j, pl.ds(0, 4 * cap), at], mate
            )
            via, out = (near_a, near_b) if h else (near_b, near_a)
            at_via, at_out = (from_a, from_b) if h else (from_b, from_a)
            copies[j, DIAG + h] = copy(j, DIAG + h, sums.at[j, 0, every, at], diag.at[j, every, at], via)
            copies[j, ONE + h] = copy(j, ONE + h, sums.at[j, 1, every, at], at_via.at[j, every, at], via)
            copies[j, TWO + h] = copy(j, TWO + h, sums.at[j, 2, every, at], at_out.at[j, every, at], out)
            if j:
                copies[j, BACK + h] = copy(
                    j, BACK + h, back.at[j, every, at], returned.at[j, every, at], others[j]
                )

    def start(j, *kinds):
        for kind in kinds:
            copies[j, kind].start()

    def arrived(j, *kinds):
        for kind in kinds:
            copies[j, kind].wait_recv()

    row_at = lax.broadcasted_iota(jnp.int32, (tok, tok), 0)
    col_at = lax.broadcasted_iota(jnp.int32, (tok, tok), 1)
    idst = idst_ref[...]
    line = lax.broadcasted_iota(jnp.int32, (16, tok), 0) ^ plane
    first, second = idst[0:1, :] == line, idst[1:2, :] == line
    named_t = jnp.where(first | second, 1.0, 0.0).astype(BF16)
    later = jnp.where(row_at < col_at, 1.0, 0.0).astype(BF16)
    rank_t = jnp.dot(named_t, later, preferred_element_type=F32)

    floats = tokens_ref[...].astype(F32)
    centered = floats - jnp.mean(floats, axis=-1, keepdims=True)
    variance = jnp.mean(centered * centered, axis=-1, keepdims=True)
    normed = (centered * lax.rsqrt(variance + 1e-05) * gain_ref[...] + bias_ref[...]).astype(BF16)
    slot_at = lax.broadcasted_iota(jnp.int32, (cap, tok), 0).astype(F32)
    for j in range(experts):
        take = (rank_t[j : j + 1, :] == slot_at) & (named_t[j : j + 1, :].astype(F32) > 0.5)
        take = jnp.where(take, 1.0, 0.0).astype(BF16)
        block = jnp.dot(take, normed, preferred_element_type=F32).astype(BF16)
        if j:
            outbox[j] = block
        else:
            rows[0, 0:cap, :] = block

    pl.semaphore_wait(barrier, len(partners))
    for j in range(1, experts):
        start(j, ZIN)
    start(0, OWN_A, OWN_B, OWN_P)

    def first_product(j, low, high):
        def tile(n, carry):
            at = pl.ds(pl.multiple_of(n * 256, 256), 256)
            acc = jnp.dot(rows[j], w_in[:, at], preferred_element_type=F32)
            hidden[:, at] = jnp.maximum(acc + b_in_ref[:, at], 0.0).astype(BF16)
            return carry

        lax.fori_loop(low, high, tile, 0)

    def second_product(j, h):
        def tile(n, carry):
            at = pl.ds(pl.multiple_of(n * 256, 256), 256)
            acc = jnp.dot(hidden[...], w_out[:, at], preferred_element_type=F32)
            part[j, :, at] = acc.astype(BF16)
            return carry

        lax.fori_loop(h * half // 256, (h + 1) * half // 256, tile, 0)

    def own(j, q, at):
        span = slice(q * cap, (q + 1) * cap)
        return part[j, span, at].astype(F32) + pair[j, span, at].astype(F32)

    def reduce_a(j, h):
        at = slice(h * half, (h + 1) * half)
        arrived(j, PAIR + h)
        sums[j, 0, :, at] = own(j, 3, at).astype(BF16)
        start(j, DIAG + h)
        sums[j, 1, :, at] = own(j, 2 - h, at).astype(BF16)
        start(j, ONE + h)

    def reduce_b(j, h):
        at = slice(h * half, (h + 1) * half)
        arrived(j, DIAG + h)
        sums[j, 2, :, at] = (own(j, 1 + h, at) + diag[j, :, at].astype(F32)).astype(BF16)
        start(j, TWO + h)

    def reduce_c(j, h):
        at = slice(h * half, (h + 1) * half)
        arrived(j, ONE + h, TWO + h)
        total = (own(j, 0, at) + from_a[j, :, at].astype(F32) + from_b[j, :, at].astype(F32)).astype(BF16)
        if j:
            back[j, :, at] = total
            start(j, BACK + h)
        else:
            returned[0, :, at] = total

    def gather_own(j):
        if j < experts:
            if j:
                arrived(j, ZIN)
            start(j, OWN_A, OWN_B, OWN_P)

    def gather_next(j):
        if j < experts:
            arrived(j, OWN_A)
            start(j, FWD_B, FWD_P1)
            arrived(j, OWN_B)
            start(j, FWD_A, FWD_P2)

    gather_own(1)
    gather_next(0)
    gather_own(2)
    tiles = hid // 256
    for j in range(experts):
        arrived(j, FWD_B, FWD_A)
        start(j, FWD_P3)
        gather_own(j + 3)
        gather_next(j + 1)
        if j == 0:
            loads[0].wait()
        arrived(j, OWN_P, FWD_P1, FWD_P2, FWD_P3)
        first_product(j, 0, tiles // 2)
        if j:
            reduce_a(j - 1, 1)
        first_product(j, tiles // 2, tiles)
        if j == 0:
            loads[1].wait()
        if j > 1:
            reduce_c(j - 2, 0)
            reduce_c(j - 2, 1)
        second_product(j, 0)
        start(j, PAIR)
        if j:
            reduce_b(j - 1, 0)
            reduce_b(j - 1, 1)
        second_product(j, 1)
        start(j, PAIR + 1)
        reduce_a(j, 0)
    last = experts - 1
    reduce_a(last, 1)
    reduce_c(last - 1, 0)
    reduce_b(last, 0)
    reduce_c(last - 1, 1)
    reduce_b(last, 1)
    reduce_c(last, 0)
    reduce_c(last, 1)

    turned = (((1,), (1,)), ((), ()))
    same = jnp.where(row_at == col_at, 1.0, 0.0)
    earlier = jnp.where(col_at < row_at, 1.0, 0.0).astype(BF16)
    named = lax.dot_general(same.astype(BF16), named_t, turned, preferred_element_type=F32)
    rank = lax.dot_general(earlier, named_t, turned, preferred_element_type=F32)
    gatest = gatest_ref[...]
    shares_t = jnp.where(first, gatest[0:1, :], 0.0) + jnp.where(second, gatest[1:2, :], 0.0)
    shares = lax.dot_general(
        same, shares_t, turned, preferred_element_type=F32, precision=lax.Precision.HIGHEST
    )
    place = lax.broadcasted_iota(jnp.int32, (tok, cap), 1).astype(F32)
    gives = []
    for j in range(experts):
        pick = (rank[:, j : j + 1] == place) & (named[:, j : j + 1] > 0.5)
        gives.append(jnp.where(pick, 1.0, 0.0).astype(BF16))
    for j in range(1, experts):
        arrived(j, BACK, BACK + 1)
    for n in range(width // 512):
        at = slice(n * 512, (n + 1) * 512)
        mixed = tokens_ref[:, at].astype(F32)
        for j in range(experts):
            value = jnp.dot(gives[j], returned[j, :, at], preferred_element_type=F32)
            mixed = mixed + shares[:, j : j + 1] * (value + b_out_ref[pl.ds(planes[j], 1), at])
        out_ref[:, at] = mixed.astype(BF16)
    for each in copies.values():
        each.wait_send()


def local(tokens, expert_ids, gate_weights, norm_gain, norm_bias, w_in, b_in, w_out, b_out):
    tok, width = tokens.shape
    top = expert_ids.shape[1]
    devices = lax.axis_size("local")
    experts = b_out.shape[0]
    shared = devices // experts
    hid = b_in.shape[1]
    cap = min(tok, shared * max(1, (3 * tok * top // (2 * experts) + shared - 1) // shared))
    cap = -(-cap // 16) * 16
    vmem = pl.BlockSpec(memory_space=pltpu.VMEM)
    hbm = pl.BlockSpec(memory_space=pl.ANY)
    return pl.pallas_call(
        functools.partial(kernel, experts, cap),
        out_shape=jax.ShapeDtypeStruct((tok, width), BF16),
        in_specs=[vmem] * 7 + [hbm] * 2,
        out_specs=vmem,
        scratch_shapes=[
            pltpu.VMEM((width, hid), BF16),
            pltpu.VMEM((hid, width), BF16),
            pltpu.VMEM((experts, 8 * cap, width), BF16),
            pltpu.VMEM((experts, cap, width), BF16),
            pltpu.VMEM((8 * cap, hid), BF16),
            pltpu.VMEM((experts, 8 * cap, width), BF16),
            pltpu.VMEM((experts, 4 * cap, width), BF16),
            pltpu.VMEM((experts, cap, width), BF16),
            pltpu.VMEM((experts, cap, width), BF16),
            pltpu.VMEM((experts, cap, width), BF16),
            pltpu.VMEM((experts, 3, cap, width), BF16),
            pltpu.VMEM((experts, cap, width), BF16),
            pltpu.VMEM((experts, cap, width), BF16),
            pltpu.SemaphoreType.DMA((2,)),
            pltpu.SemaphoreType.DMA((experts * KINDS,)),
            pltpu.SemaphoreType.DMA((experts * KINDS,)),
        ],
        compiler_params=pltpu.CompilerParams(
            collective_id=0, has_side_effects=True, vmem_limit_bytes=64 * 1024 * 1000
        ),
    )(
        tokens, expert_ids.T, gate_weights.T, norm_gain[None, :], norm_bias[None, :], b_in, b_out, w_in, w_out,
    )


def solution(mesh):
    in_specs = (
        P(("groups", "local"), None),
        P(("groups", "local"), None),
        P(("groups", "local"), None),
        P(),
        P(),
        P("local", None, None),
        P("local", None),
        P("local", None, None),
        P(),
    )
    out_specs = P(("groups", "local"), None)
    return jax.shard_map(local, mesh=mesh, in_specs=in_specs, out_specs=out_specs, check_vma=False)
```

profile of v0, /device:TPU:0, one launch (start us, length us, event | category | flops | bytes accessed | tf_op | source)
XLA Modules:
  0.0 77.9 jit_solution(10424501586850472346)
XLA Ops:
  0.0 76.2 %shard_map.91 = bf16[64,2048]{1,0:T(8,128)(2,1)} custom-call(bf16[64,2048]{1,0:T(8,128)(2,1)} %tokens_ref.1, s32[2,64]{1,0:T(2,128)} %bitcast.6, f32[2,64]{1,0:T(2,128)} %bitcast.7, f32[1,2048]{1,0:T(1,128)} %bitcast.4, f32[1,2048]{1,0:T(1,128)} %bitcast.5, f32[1,1024]{1,0:T(1,128)} %b_in_ref.1, f32[4,2048]{1,0:T(4,128)} %b_out_ref.1, ...), custom_call_target="tpu_custom_call" | custom-call | tf_op jit(solution)/shard_map/pallas_call | solution.py:274
  76.2 1.7 %copy.11 = bf16[64,2048]{1,0:T(8,128)(2,1)} copy(bf16[64,2048]{1,0:T(8,128)(2,1)} %shard_map.91) | data formatting | bytes 524288
where the time goes:
time: 79.4 us; the launch traced here: 77.9 us
  Pallas kernels  76.2 us (96%)
  local copies, waits for them, and re-layouts  1.67 us (2%)
    pallas_call x1, Pallas kernels, local(): pl.pallas_call(functools.partial(kernel, experts, cap), out_shape=jax.Sha...  76.2 us
    unnamed x1, local copies, waits for them, and re-layouts  1.67 us

commit v1 on v0

--- a/solution.py
+++ b/solution.py
@@ -10,9 +10,9 @@
 MESH = pl.DeviceIdType.MESH
 F32 = jnp.float32
 BF16 = jnp.bfloat16
-ZIN, OWN_A, OWN_B, OWN_P, FWD_B, FWD_P1, FWD_P2, FWD_P3, FWD_A = range(9)
-PAIR, DIAG, ONE, TWO, BACK = 9, 11, 13, 15, 17
-KINDS = 19
+ZIN, OWN_A, REST_A, OWN_B, REST_B, OWN_P, FWD_B, FWD_P1, FWD_P2, FWD_P3, FWD_A = range(11)
+PAIR, DIAG, ONE, TWO, BACK = 11, 13, 15, 17, 19
+KINDS = 21
 
 
 def xor_with(value, fixed, limit):
@@ -74,10 +74,12 @@
     for j in range(experts):
         if j:
             copies[j, ZIN] = copy(j, ZIN, outbox.at[j], chunk(j, 0), others[j])
-        copies[j, OWN_A] = copy(j, OWN_A, chunk(j, 0), chunk(j, 1), near_a)
-        copies[j, OWN_B] = copy(j, OWN_B, chunk(j, 0), chunk(j, 2), near_b)
+        low, high = pl.ds(0, half), pl.ds(half, half)
+        copies[j, OWN_A] = copy(j, OWN_A, piece(j, 0, low), piece(j, 1, low), near_a)
+        copies[j, REST_A] = copy(j, REST_A, piece(j, 0, high), piece(j, 1, high), near_a)
+        copies[j, OWN_B] = copy(j, OWN_B, piece(j, 0, high), piece(j, 2, high), near_b)
+        copies[j, REST_B] = copy(j, REST_B, piece(j, 0, low), piece(j, 2, low), near_b)
         copies[j, OWN_P] = copy(j, OWN_P, chunk(j, 0), chunk(j, 4), mate)
-        low, high = pl.ds(0, half), pl.ds(half, half)
         copies[j, FWD_B] = copy(j, FWD_B, piece(j, 1, low), piece(j, 3, low), near_b)
         copies[j, FWD_A] = copy(j, FWD_A, piece(j, 2, high), piece(j, 3, high), near_a)
         copies[j, FWD_P1] = copy(j, FWD_P1, chunk(j, 1), chunk(j, 5), mate)
@@ -131,9 +133,9 @@
             rows[0, 0:cap, :] = block
 
     pl.semaphore_wait(barrier, len(partners))
-    for j in range(1, experts):
+    for j in range(1, min(3, experts)):
         start(j, ZIN)
-    start(0, OWN_A, OWN_B, OWN_P)
+    start(0, OWN_A, OWN_B, REST_A, REST_B, OWN_P)
 
     def first_product(j, low, high):
         def tile(n, carry):
@@ -183,54 +185,96 @@
 
     def gather_own(j):
         if j < experts:
-            if j:
-                arrived(j, ZIN)
-            start(j, OWN_A, OWN_B, OWN_P)
+            arrived(j, ZIN)
+            start(j, OWN_A, OWN_B, REST_A, REST_B, OWN_P)
+            if j + 2 < experts:
+                start(j + 2, ZIN)
 
     def gather_next(j):
         if j < experts:
             arrived(j, OWN_A)
-            start(j, FWD_B, FWD_P1)
+            start(j, FWD_B)
             arrived(j, OWN_B)
-            start(j, FWD_A, FWD_P2)
-
+            start(j, FWD_A)
+
+    def gather_mate(j):
+        if j < experts:
+            arrived(j, REST_A)
+            start(j, FWD_P1)
+            arrived(j, REST_B)
+            start(j, FWD_P2)
+
+    def gather_last(j):
+        if j < experts:
+            arrived(j, FWD_B, FWD_A)
+            start(j, FWD_P3)
+
+    gather_next(0)
     gather_own(1)
-    gather_next(0)
-    gather_own(2)
+    gather_mate(0)
+    gather_last(0)
     tiles = hid // 256
+    last = experts - 1
     for j in range(experts):
-        arrived(j, FWD_B, FWD_A)
-        start(j, FWD_P3)
-        gather_own(j + 3)
-        gather_next(j + 1)
         if j == 0:
             loads[0].wait()
+        else:
+            gather_next(j + 1)
         arrived(j, OWN_P, FWD_P1, FWD_P2, FWD_P3)
+        if j > 2:
+            reduce_a(j - 1, 0)
         first_product(j, 0, tiles // 2)
-        if j:
+        if j == 0:
+            gather_next(1)
+        if j == 2:
+            reduce_a(1, 0)
+        if j > 2:
             reduce_a(j - 1, 1)
         first_product(j, tiles // 2, tiles)
         if j == 0:
             loads[1].wait()
+        gather_own(j + 2)
         if j > 1:
+            gather_mate(j + 1)
+        if j == 3:
+            reduce_b(1, 0)
+        second_product(j, 0)
+        start(j, PAIR)
+        if j > 1:
+            gather_last(j + 1)
+        else:
+            gather_mate(j + 1)
+        if j == 2:
+            reduce_a(1, 1)
+        if j > 2:
+            reduce_b(j - 1, 0)
+        if j == 3:
+            reduce_b(1, 1)
+        second_product(j, 1)
+        start(j, PAIR + 1)
+        if j < 2:
+            gather_last(j + 1)
+        if j > 2:
+            reduce_b(j - 1, 1)
+        if j > 3:
             reduce_c(j - 2, 0)
             reduce_c(j - 2, 1)
-        second_product(j, 0)
-        start(j, PAIR)
-        if j:
-            reduce_b(j - 1, 0)
-            reduce_b(j - 1, 1)
-        second_product(j, 1)
-        start(j, PAIR + 1)
-        reduce_a(j, 0)
-    last = experts - 1
+    reduce_a(last, 0)
     reduce_a(last, 1)
     reduce_c(last - 1, 0)
+    reduce_a(0, 0)
+    reduce_c(last - 1, 1)
     reduce_b(last, 0)
-    reduce_c(last - 1, 1)
     reduce_b(last, 1)
+    reduce_a(0, 1)
+    reduce_c(1, 0)
+    reduce_c(1, 1)
     reduce_c(last, 0)
+    reduce_b(0, 0)
     reduce_c(last, 1)
+    reduce_b(0, 1)
+    reduce_c(0, 0)
+    reduce_c(0, 1)
 
     turned = (((1,), (1,)), ((), ()))
     same = jnp.where(row_at == col_at, 1.0, 0.0)

time: 79.4 us -> 70.8 us (0.89); the launches traced: 77.9 us -> 70.6 us
  Pallas kernels: 76.2 us -> 69 us
    pallas_call x1, Pallas kernels: 76.2 us -> 69 us  [local(): pl.pallas_call(functools.partial(kernel, experts, cap), out_shape=jax.Sha...]
where the time goes in v1:
time: 70.8 us; the launch traced here: 70.6 us
  Pallas kernels  69 us (97%)
  local copies, waits for them, and re-layouts  1.67 us (2%)
    pallas_call x1, Pallas kernels, local(): pl.pallas_call(functools.partial(kernel, experts, cap), out_shape=jax.Sha...  69 us
    unnamed x1, local copies, waits for them, and re-layouts  1.67 us

profile of v1, /device:TPU:0, one launch (start us, length us, event | category | flops | bytes accessed | tf_op | source)
XLA Modules:
  0.0 70.6 jit_solution(12089693448498275811)
XLA Ops:
  0.0 69.0 %shard_map.91 = bf16[64,2048]{1,0:T(8,128)(2,1)} custom-call(bf16[64,2048]{1,0:T(8,128)(2,1)} %tokens_ref.1, s32[2,64]{1,0:T(2,128)} %bitcast.6, f32[2,64]{1,0:T(2,128)} %bitcast.7, f32[1,2048]{1,0:T(1,128)} %bitcast.4, f32[1,2048]{1,0:T(1,128)} %bitcast.5, f32[1,1024]{1,0:T(1,128)} %b_in_ref.1, f32[4,2048]{1,0:T(4,128)} %b_out_ref.1, ...), custom_call_target="tpu_custom_call" | custom-call | tf_op jit(solution)/shard_map/pallas_call | solution.py:318
  69.0 1.7 %copy.11 = bf16[64,2048]{1,0:T(8,128)(2,1)} copy(bf16[64,2048]{1,0:T(8,128)(2,1)} %shard_map.91) | data formatting | bytes 524288

commit v2 on v1

--- a/solution.py
+++ b/solution.py
@@ -146,26 +146,33 @@
 
         lax.fori_loop(low, high, tile, 0)
 
-    def second_product(j, h):
+    def second_product(j, low, high):
         def tile(n, carry):
             at = pl.ds(pl.multiple_of(n * 256, 256), 256)
             acc = jnp.dot(hidden[...], w_out[:, at], preferred_element_type=F32)
             part[j, :, at] = acc.astype(BF16)
             return carry
 
-        lax.fori_loop(h * half // 256, (h + 1) * half // 256, tile, 0)
+        lax.fori_loop(low, high, tile, 0)
 
     def own(j, q, at):
         span = slice(q * cap, (q + 1) * cap)
         return part[j, span, at].astype(F32) + pair[j, span, at].astype(F32)
 
-    def reduce_a(j, h):
+    def reduce_d(j, h):
         at = slice(h * half, (h + 1) * half)
         arrived(j, PAIR + h)
         sums[j, 0, :, at] = own(j, 3, at).astype(BF16)
         start(j, DIAG + h)
+
+    def reduce_o(j, h):
+        at = slice(h * half, (h + 1) * half)
         sums[j, 1, :, at] = own(j, 2 - h, at).astype(BF16)
         start(j, ONE + h)
+
+    def reduce_a(j, h):
+        reduce_d(j, h)
+        reduce_o(j, h)
 
     def reduce_b(j, h):
         at = slice(h * half, (h + 1) * half)
@@ -214,62 +221,75 @@
     gather_mate(0)
     gather_last(0)
     tiles = hid // 256
+    wide = half // 256
     last = experts - 1
     for j in range(experts):
         if j == 0:
             loads[0].wait()
+        if j == 1:
+            gather_next(2)
+        arrived(j, OWN_P, FWD_P1, FWD_P2, FWD_P3)
+        first_product(j, 0, tiles // 2)
+        if j != 1:
+            gather_next(j + 1)
         else:
-            gather_next(j + 1)
-        arrived(j, OWN_P, FWD_P1, FWD_P2, FWD_P3)
-        if j > 2:
-            reduce_a(j - 1, 0)
-        first_product(j, 0, tiles // 2)
-        if j == 0:
-            gather_next(1)
-        if j == 2:
-            reduce_a(1, 0)
+            gather_own(3)
         if j > 2:
             reduce_a(j - 1, 1)
         first_product(j, tiles // 2, tiles)
         if j == 0:
             loads[1].wait()
-        gather_own(j + 2)
-        if j > 1:
-            gather_mate(j + 1)
-        if j == 3:
-            reduce_b(1, 0)
-        second_product(j, 0)
-        start(j, PAIR)
-        if j > 1:
-            gather_last(j + 1)
+            gather_own(2)
         else:
             gather_mate(j + 1)
         if j == 2:
-            reduce_a(1, 1)
+            reduce_a(1, 0)
+        if j == 3:
+            reduce_b(1, 0)
         if j > 2:
             reduce_b(j - 1, 0)
-        if j == 3:
-            reduce_b(1, 1)
-        second_product(j, 1)
-        start(j, PAIR + 1)
-        if j < 2:
-            gather_last(j + 1)
+        second_product(j, 0, wide)
+        start(j, PAIR)
+        if j == 0:
+            gather_mate(1)
+        if j == 1:
+            gather_last(2)
+            reduce_d(0, 0)
+        if j == 2:
+            reduce_d(1, 1)
+        if j > 1:
+            gather_own(j + 2)
         if j > 2:
             reduce_b(j - 1, 1)
-        if j > 3:
-            reduce_c(j - 2, 0)
-            reduce_c(j - 2, 1)
+        if j == 3:
+            reduce_o(1, 1)
+            reduce_b(1, 1)
+        second_product(j, wide, 3 * wide // 2)
+        if j > 1:
+            gather_last(j + 1)
+        second_product(j, 3 * wide // 2, 2 * wide)
+        start(j, PAIR + 1)
+        if j == 0:
+            gather_last(1)
+        if j > 1 and j < last:
+            reduce_a(j, 0)
+        if j > 2:
+            reduce_c(j - 1, 0)
+            if j < last:
+                reduce_c(j - 1, 1)
     reduce_a(last, 0)
-    reduce_a(last, 1)
-    reduce_c(last - 1, 0)
-    reduce_a(0, 0)
-    reduce_c(last - 1, 1)
+    if last > 2:
+        reduce_c(last - 1, 1)
+    reduce_d(last, 1)
+    reduce_o(0, 0)
+    reduce_c(1, 0)
     reduce_b(last, 0)
+    reduce_o(last, 1)
     reduce_b(last, 1)
-    reduce_a(0, 1)
-    reduce_c(1, 0)
     reduce_c(1, 1)
+    reduce_d(0, 1)
     reduce_c(last, 0)
+    reduce_o(0, 1)
     reduce_b(0, 0)
     reduce_c(last, 1)
     reduce_b(0, 1)

time: 70.8 us -> 69.2 us (0.977)
  Pallas kernels: 69 us -> 67.3 us
    pallas_call x1, Pallas kernels: 69 us -> 67.3 us  [local(): pl.pallas_call(functools.partial(kernel, experts, cap), out_shape=jax.Sha...]
where the time goes in v2:
time: 69.2 us; the launch traced here: 69 us
  Pallas kernels  67.3 us (97%)
  local copies, waits for them, and re-layouts  1.67 us (2%)
    pallas_call x1, Pallas kernels, local(): pl.pallas_call(functools.partial(kernel, experts, cap), out_shape=jax.Sha...  67.3 us
    unnamed x1, local copies, waits for them, and re-layouts  1.67 us

profile of v2, /device:TPU:0, one launch (start us, length us, event | category | flops | bytes accessed | tf_op | source)
XLA Modules:
  0.0 69.0 jit_solution(2680050635784709597)
XLA Ops:
  0.0 67.3 %shard_map.91 = bf16[64,2048]{1,0:T(8,128)(2,1)} custom-call(bf16[64,2048]{1,0:T(8,128)(2,1)} %tokens_ref.1, s32[2,64]{1,0:T(2,128)} %bitcast.6, f32[2,64]{1,0:T(2,128)} %bitcast.7, f32[1,2048]{1,0:T(1,128)} %bitcast.4, f32[1,2048]{1,0:T(1,128)} %bitcast.5, f32[1,1024]{1,0:T(1,128)} %b_in_ref.1, f32[4,2048]{1,0:T(4,128)} %b_out_ref.1, ...), custom_call_target="tpu_custom_call" | custom-call | tf_op jit(solution)/shard_map/pallas_call | solution.py:338
  67.4 1.7 %copy.11 = bf16[64,2048]{1,0:T(8,128)(2,1)} copy(bf16[64,2048]{1,0:T(8,128)(2,1)} %shard_map.91) | data formatting | bytes 524288
